TPU v7x, 1024 devices: a whole 4x4x32 slice. The times are simulated.
1024 devices in a mesh: blk: 128 (over y, z_lo, core), ulysses: 8 (over z_hi, x).
Axes of the slice: x: 4, y: 4, z: 32 (z_hi: 2, z_lo: 16; z = z_hi * 16 + z_lo), core: 2. Of those that a mesh axis runs over, the one named last changes fastest.
Arguments:
- queries: bfloat16 [131072, 2048], P(('blk', 'ulysses')), may hold values from -6 to 6
- key_states: bfloat16 [131072, 512], P(('blk', 'ulysses')), may hold values from -6 to 6
- value_states: bfloat16 [131072, 512], P(('blk', 'ulysses')), may hold values from -6 to 6
- attn_out: bfloat16 [131072, 2048], P(('blk', 'ulysses')), may hold values from -6 to 6
- grad_out: bfloat16 [131072, 2048], P(('blk', 'ulysses')), may hold values from -6 to 6
- log_sums: float32 [131072, 32], P(('blk', 'ulysses')), may hold values from 2 to 4
- owners: int32 [256], replicated, may hold values from 0 to 255, as said below
Outputs:
- grad_query: bfloat16 [131072, 2048], P(('blk', 'ulysses'))
- grad_key: bfloat16 [131072, 512], P(('blk', 'ulysses'))
- grad_value: bfloat16 [131072, 512], P(('blk', 'ulysses'))
Inputs may be any that keep to these rules, and one draw needn't show every extreme that they name: `owners`: every value 0 to 255 appears exactly once; each sequence block holds one half-block below 128 and the half-block 2 * 128 - 1 minus it.
All inputs are finite; a program needn't handle non-finite values.
Results may differ from a plain program's by a relative error of at most 0.0049.
Values may be sent and summed in bfloat16 or wider, within the bound.
A program may use at most 32 MiB of HBM per device.

v0:
```python
import math

import jax
import jax.numpy as jnp
from jax import lax
from jax.sharding import PartitionSpec as P

HEAD_DIM = 64


def from_behind(value, axis, steps):
    count = lax.axis_size(axis)
    pairs = [(source, (source + steps) % count) for source in range(count)]
    return lax.ppermute(value, axis, pairs)


def block_grads(query_blk, grad_blk, key_blk, value_blk, sums_blk, delta_blk, query_pos, key_pos):
    wide = jnp.float32
    count = query_blk.shape[0]
    kv_local = key_blk.shape[1] // HEAD_DIM
    heads_local = sums_blk.shape[1]
    group = heads_local // kv_local
    factor = 1.0 / math.sqrt(HEAD_DIM)
    query_x = query_blk.reshape(count, kv_local, group, HEAD_DIM)
    grad_x = grad_blk.reshape(count, kv_local, group, HEAD_DIM)
    key_x = key_blk.reshape(count, kv_local, HEAD_DIM)
    value_x = value_blk.reshape(count, kv_local, HEAD_DIM)
    sums_t = jnp.transpose(sums_blk.reshape(count, kv_local, group), (2, 1, 0))[..., None]
    delta_t = jnp.transpose(delta_blk.reshape(count, kv_local, group), (2, 1, 0))[..., None]
    visible = query_pos[:, None] >= key_pos[None, :]

    def one_head(carry, member):
        key_acc, value_acc = carry
        query_one = lax.dynamic_index_in_dim(query_x, member, 2, keepdims=False)
        grad_one = lax.dynamic_index_in_dim(grad_x, member, 2, keepdims=False)
        sums_one = lax.dynamic_index_in_dim(sums_t, member, 0, keepdims=False)
        delta_one = lax.dynamic_index_in_dim(delta_t, member, 0, keepdims=False)
        scores = jnp.einsum("qhd,khd->hqk", query_one, key_x, preferred_element_type=wide) * factor
        probs = jnp.where(visible, jnp.exp(scores - sums_one), 0.0)
        probs_b = probs.astype(jnp.bfloat16)
        value_acc = value_acc + jnp.einsum(
            "hqk,qhd->khd", probs_b, grad_one, preferred_element_type=wide
        )
        dprobs = jnp.einsum("qhd,khd->hqk", grad_one, value_x, preferred_element_type=wide)
        dscores = (probs * (dprobs - delta_one) * factor).astype(jnp.bfloat16)
        query_piece = jnp.einsum("hqk,khd->qhd", dscores, key_x, preferred_element_type=wide)
        key_acc = key_acc + jnp.einsum(
            "hqk,qhd->khd", dscores, query_one, preferred_element_type=wide
        )
        return ((key_acc, value_acc), query_piece.astype(jnp.bfloat16))

    empty = jnp.zeros((count, kv_local, HEAD_DIM), wide)
    (grad_key, grad_value), pieces = lax.scan(
        one_head, (empty, empty), jnp.arange(group, dtype=jnp.int32)
    )
    grad_query = jnp.transpose(pieces, (1, 2, 0, 3))
    return (
        grad_query.reshape(count, -1),
        grad_key.astype(jnp.bfloat16).reshape(count, -1),
        grad_value.astype(jnp.bfloat16).reshape(count, -1),
    )


def send_back(grad_key, grad_value):
    stacked = from_behind(jnp.stack([grad_key, grad_value]), "blk", -1)
    return (stacked[0], stacked[1])


def per_device(queries, key_states, value_states, attn_out, grad_out, log_sums, owners):
    tok_rows = queries.shape[0]
    heads_all = log_sums.shape[1]
    delta = jnp.sum(
        (grad_out.astype(jnp.float32) * attn_out.astype(jnp.float32)).reshape(
            tok_rows, heads_all, HEAD_DIM
        ),
        axis=2,
    )
    sums_h, delta_h = (
        lax.all_to_all(log_sums, "ulysses", split_axis=1, concat_axis=0, tiled=True),
        lax.all_to_all(delta, "ulysses", split_axis=1, concat_axis=0, tiled=True),
    )
    query_h, grad_h, key_h, value_h = (
        lax.all_to_all(queries, "ulysses", split_axis=1, concat_axis=0, tiled=True),
        lax.all_to_all(grad_out, "ulysses", split_axis=1, concat_axis=0, tiled=True),
        lax.all_to_all(key_states, "ulysses", split_axis=1, concat_axis=0, tiled=True),
        lax.all_to_all(value_states, "ulysses", split_axis=1, concat_axis=0, tiled=True),
    )
    moved = from_behind(jnp.stack([key_h, value_h]), "blk", 1)
    key_prev, value_prev = (moved[0], moved[1])
    group_tok = query_h.shape[0]
    half = group_tok // 2
    rank = lax.axis_index("blk")
    before = (rank - 1) % lax.axis_size("blk")
    offsets = jnp.arange(group_tok, dtype=jnp.int32)
    query_pos = jnp.take(owners, 2 * rank + offsets // half) * half + offsets % half
    key_pos = jnp.take(owners, 2 * before + offsets // half) * half + offsets % half
    grad_query, grad_key, grad_value = block_grads(
        query_h, grad_h, key_prev, value_prev, sums_h, delta_h, query_pos, key_pos
    )
    key_back, value_back = send_back(grad_key, grad_value)
    out_query, out_key, out_value = (
        lax.all_to_all(grad_query, "ulysses", split_axis=0, concat_axis=1, tiled=True),
        lax.all_to_all(key_back, "ulysses", split_axis=0, concat_axis=1, tiled=True),
        lax.all_to_all(value_back, "ulysses", split_axis=0, concat_axis=1, tiled=True),
    )
    return (out_query, out_key, out_value)


def solution(mesh):
    return jax.shard_map(
        per_device,
        mesh=mesh,
        in_specs=(
            P(("blk", "ulysses"), None),
            P(("blk", "ulysses"), None),
            P(("blk", "ulysses"), None),
            P(("blk", "ulysses"), None),
            P(("blk", "ulysses"), None),
            P(("blk", "ulysses"), None),
            P(),
        ),
        out_specs=(
            P(("blk", "ulysses"), None),
            P(("blk", "ulysses"), None),
            P(("blk", "ulysses"), None),
        ),
        check_vma=False,
    )
```

profile of v0, /device:TPU:57, one launch (start us, length us, event | category | flops | bytes accessed | tf_op | source)
XLA Modules:
  0.0 413.9 jit_solution(1958582542821395017)
XLA Ops:
  0.7 29.8 %all-to-all-start.3 = ((f32[128,8,4]{0,2,1:T(4,128)}), f32[128,8,4]{0,2,1:T(4,128)S(1)}, u32[]{:S(2)}, u32[]{:S(2)}) async-start(f32[128,8,4]{0,2,1:T(4,128)} %bitcast.165), calls=%async_computation.3 | async-start | bytes 32768 | tf_op jit(solution)/shard_map/all_to_all | solution.py:79
  30.4 1.7 copy.61
  32.1 21.7 %all-to-all-done.3 = f32[128,8,4]{0,2,1:T(4,128)S(1)} async-done(((f32[128,8,4]{0,2,1:T(4,128)}), f32[128,8,4]{0,2,1:T(4,128)S(1)}, u32[]{:S(2)}, u32[]{:S(2)}) %all-to-all-start.3) | async-done | bytes 16416 | tf_op jit(solution)/shard_map/all_to_all | solution.py:79
  53.8 3.4 all-to-all-start.1
  57.2 1.7 copy.63
  58.9 22.0 %all-to-all-done.1 = bf16[128,8,64]{0,2,1:T(8,128)(2,1)S(1)} async-done(((bf16[128,8,64]{0,2,1:T(8,128)(2,1)}), bf16[128,8,64]{0,2,1:T(8,128)(2,1)S(1)}, u32[]{:S(2)}, u32[]{:S(2)}) %all-to-all-start.1) | async-done | bytes 131104 | tf_op jit(solution)/shard_map/all_to_all | solution.py:85
  80.9 3.4 all-to-all-start.2
  84.3 2.1 copy.65
  86.3 21.6 %all-to-all-done.2 = bf16[128,8,64]{0,2,1:T(8,128)(2,1)S(1)} async-done(((bf16[128,8,64]{0,2,1:T(8,128)(2,1)}), bf16[128,8,64]{0,2,1:T(8,128)(2,1)S(1)}, u32[]{:S(2)}, u32[]{:S(2)}) %all-to-all-start.2) | async-done | bytes 131104 | tf_op jit(solution)/shard_map/all_to_all | solution.py:86
  108.0 3.5 all-to-all-start.4
  111.5 2.0 copy.59
  113.5 59.2 %all-to-all-done.4 = bf16[128,8,256]{0,2,1:T(8,128)(2,1)S(1)} async-done(((bf16[128,8,256]{0,2,1:T(8,128)(2,1)}), bf16[128,8,256]{0,2,1:T(8,128)(2,1)S(1)}, u32[]{:S(2)}, u32[]{:S(2)}) %all-to-all-start.4) | async-done | bytes 524320 | tf_op jit(solution)/shard_map/all_to_all | solution.py:84
  172.7 3.7 all-to-all-start
  176.7 1.9 bitcast_reduce_fusion
  178.9 1.9 collective-permute-start
  180.9 6.9 %gather_fusion = s32[1024]{0:T(1024)S(1)} fusion(s32[256]{0:T(256)S(1)} %copy-done, s32[1024]{0:T(1024)S(1)} %fusion.43), kind=kCustom, calls=%fused_computation.1.clone | custom fusion | bytes 12288 | tf_op jit(solution)/shard_map/jit(_take)/gather | solution.py:96
  187.7 6.9 %gather_fusion.1 = s32[1024]{0:T(1024)S(1)} fusion(s32[256]{0:T(256)S(1)} %copy-done, s32[1024]{0:T(1024)S(1)} %fusion.44), kind=kCustom, calls=%fused_computation.clone | custom fusion | bytes 12288 | tf_op jit(solution)/shard_map/jit(_take)/gather | solution.py:95
  194.6 25.4 %all-to-all-done = bf16[128,8,256]{0,2,1:T(8,128)(2,1)S(1)} async-done(((bf16[128,8,256]{0,2,1:T(8,128)(2,1)}), bf16[128,8,256]{0,2,1:T(8,128)(2,1)S(1)}, u32[]{:S(2)}, u32[]{:S(2)}) %all-to-all-start) | async-done | bytes 524320 | tf_op jit(solution)/shard_map/all_to_all | solution.py:83
  220.0 7.6 %all-to-all-start.5 = ((f32[128,8,4]{0,2,1:T(4,128)}), f32[128,8,4]{0,2,1:T(4,128)S(1)}, u32[]{:S(2)}, u32[]{:S(2)}) async-start(f32[128,8,4]{0,2,1:T(4,128)} %bitcast.16), calls=%async_computation.5 | async-start | bytes 32768 | tf_op jit(solution)/shard_map/all_to_all | solution.py:80
  228.8 22.2 %all-to-all-done.5 = f32[128,8,4]{0,2,1:T(4,128)S(1)} async-done(((f32[128,8,4]{0,2,1:T(4,128)}), f32[128,8,4]{0,2,1:T(4,128)S(1)}, u32[]{:S(2)}, u32[]{:S(2)}) %all-to-all-start.5) | async-done | bytes 16416 | tf_op jit(solution)/shard_map/all_to_all | solution.py:80
  251.0 30.5 %while.15 = (s32[]{:T(128)}, f32[1024,1,64]{0,2,1:T(8,128)S(1)}, f32[1024,1,64]{0,2,1:T(8,128)S(1)}, bf16[4,1024,1,64]{1,3,2,0:T(8,128)(2,1)S(1)}, s32[4]{0:T(12...) while((s32[]{:T(128)}, f32[1024,1,64]{0,2,1:T(8,128)S(1)}, ...), condition=%wide.region_2.4_spmd.clone, body=%wide.region_1.3_spmd.clone.sunk | while | flops 685047808 | bytes 21016812 | solution.py:53
  255.4 1.9 multiply_convert_fusion.2
  263.1 1.9 multiply_convert_fusion.2
  270.7 1.9 multiply_convert_fusion.2
  278.3 1.9 multiply_convert_fusion.2
  281.6 17.6 %collective-permute-start.1 = (bf16[2,1024,64]{1,2,0:T(8,128)(2,1)S(1)}, bf16[2,1024,64]{1,2,0:T(8,128)(2,1)S(1)}, u32[]{:S(2)}, u32[]{:S(2)}) collective-permute-start(bf16[2,1024,64]{1,2,0:T(8,128)(2,1)S(1)} %pad_maximum_fusion.1), channel_id=1, source_target_pairs={{0,1016},{8,0},{16,8},{24,16},{32,24},{40,32},{48,40},{56,48},{64,... | collective-permute-start | bytes 786440 | tf_op jit(solution)/shard_map/ppermute | solution.py:14
  301.1 3.4 all-to-all-start.8
  305.2 23.0 %all-to-all-done.8 = bf16[8,128,64]{1,2,0:T(8,128)(2,1)S(1)} async-done(((bf16[8,128,64]{1,2,0:T(8,128)(2,1)}), bf16[8,128,64]{1,2,0:T(8,128)(2,1)S(1)}, u32[]{:S(2)}, u32[]{:S(2)}) %all-to-all-start.8) | async-done | bytes 131104 | tf_op jit(solution)/shard_map/all_to_all | solution.py:104
  328.2 3.4 all-to-all-start.7
  332.8 22.6 %all-to-all-done.7 = bf16[8,128,64]{1,2,0:T(8,128)(2,1)S(1)} async-done(((bf16[8,128,64]{1,2,0:T(8,128)(2,1)}), bf16[8,128,64]{1,2,0:T(8,128)(2,1)S(1)}, u32[]{:S(2)}, u32[]{:S(2)}) %all-to-all-start.7) | async-done | bytes 131104 | tf_op jit(solution)/shard_map/all_to_all | solution.py:103
  355.4 4.6 %all-to-all-start.6 = ((bf16[8,128,256]{2,1,0:T(8,128)(2,1)}), bf16[8,128,256]{2,1,0:T(8,128)(2,1)S(1)}, u32[]{:S(2)}, u32[]{:S(2)}) async-start(bf16[8,128,256]{2,1,0:T(8,128)(2,1)} %copy.71), calls=%async_computation.6 | async-start | bytes 1048576 | tf_op jit(solution)/shard_map/all_to_all | solution.py:102
  361.5 51.1 %all-to-all-done.6 = bf16[8,128,256]{2,1,0:T(8,128)(2,1)S(1)} async-done(((bf16[8,128,256]{2,1,0:T(8,128)(2,1)}), bf16[8,128,256]{2,1,0:T(8,128)(2,1)S(1)}, u32[]{:S(2)}, u32[]{:S(2)}) %all-to-all-start.6) | async-done | bytes 524320 | tf_op jit(solution)/shard_map/all_to_all | solution.py:102
  (62 shorter events, 23.3 us)
Async XLA Ops:
  0.6 180.2 %copy-start = (s32[256]{0:T(256)S(1)}, s32[256]{0:T(256)}, u32[]{:S(2)}) copy-start(s32[256]{0:T(256)} %param.17) | copy-start | bytes 3076
  0.6 175.7 %copy-start.1 = (bf16[128,2048]{1,0:T(8,128)(2,1)S(1)}, bf16[128,2048]{1,0:T(8,128)(2,1)}, u32[]{:S(2)}) copy-start(bf16[128,2048]{1,0:T(8,128)(2,1)} %param.14) | copy-start | bytes 1572868
  0.7 53.2 %all-to-all-start.3 = ((f32[128,8,4]{0,2,1:T(4,128)}), f32[128,8,4]{0,2,1:T(4,128)S(1)}, u32[]{:S(2)}, u32[]{:S(2)}) async-start(f32[128,8,4]{0,2,1:T(4,128)} %bitcast.165), calls=%async_computation.3 | async-start | bytes 32768 | tf_op jit(solution)/shard_map/all_to_all | solution.py:79
  53.8 27.1 %all-to-all-start.1 = ((bf16[128,8,64]{0,2,1:T(8,128)(2,1)}), bf16[128,8,64]{0,2,1:T(8,128)(2,1)S(1)}, u32[]{:S(2)}, u32[]{:S(2)}) async-start(bf16[128,8,64]{0,2,1:T(8,128)(2,1)} %bitcast.2), calls=%async_computation.1 | async-start | bytes 262144 | tf_op jit(solution)/shard_map/all_to_all | solution.py:85
  80.9 27.1 %all-to-all-start.2 = ((bf16[128,8,64]{0,2,1:T(8,128)(2,1)}), bf16[128,8,64]{0,2,1:T(8,128)(2,1)S(1)}, u32[]{:S(2)}, u32[]{:S(2)}) async-start(bf16[128,8,64]{0,2,1:T(8,128)(2,1)} %bitcast.4), calls=%async_computation.2 | async-start | bytes 262144 | tf_op jit(solution)/shard_map/all_to_all | solution.py:86
  108.0 64.7 %all-to-all-start.4 = ((bf16[128,8,256]{0,2,1:T(8,128)(2,1)}), bf16[128,8,256]{0,2,1:T(8,128)(2,1)S(1)}, u32[]{:S(2)}, u32[]{:S(2)}) async-start(bf16[128,8,256]{0,2,1:T(8,128)(2,1)} %bitcast.12), calls=%async_computation.4 | async-start | bytes 1048576 | tf_op jit(solution)/shard_map/all_to_all | solution.py:84
  172.7 47.4 %all-to-all-start = ((bf16[128,8,256]{0,2,1:T(8,128)(2,1)}), bf16[128,8,256]{0,2,1:T(8,128)(2,1)S(1)}, u32[]{:S(2)}, u32[]{:S(2)}) async-start(bf16[128,8,256]{0,2,1:T(8,128)(2,1)} %bitcast), calls=%async_computation | async-start | bytes 1048576 | tf_op jit(solution)/shard_map/all_to_all | solution.py:83
  178.9 48.8 %collective-permute-start = (bf16[2,1024,64]{1,2,0:T(8,128)(2,1)S(1)}, bf16[2,1024,64]{1,2,0:T(8,128)(2,1)S(1)}, u32[]{:S(2)}, u32[]{:S(2)}) collective-permute-start(bf16[2,1024,64]{1,2,0:T(8,128)(2,1)S(1)} %pad_maximum_fusion), channel_id=1, source_target_pairs={{0,8},{8,16},{16,24},{24,32},{32,40},{40,48},{48,56},{56,64},{64,7... | collective-permute-start | bytes 786440 | tf_op jit(solution)/shard_map/ppermute | solution.py:14
  220.0 31.0 %all-to-all-start.5 = ((f32[128,8,4]{0,2,1:T(4,128)}), f32[128,8,4]{0,2,1:T(4,128)S(1)}, u32[]{:S(2)}, u32[]{:S(2)}) async-start(f32[128,8,4]{0,2,1:T(4,128)} %bitcast.16), calls=%async_computation.5 | async-start | bytes 32768 | tf_op jit(solution)/shard_map/all_to_all | solution.py:80
  281.6 18.7 %collective-permute-start.1 = (bf16[2,1024,64]{1,2,0:T(8,128)(2,1)S(1)}, bf16[2,1024,64]{1,2,0:T(8,128)(2,1)S(1)}, u32[]{:S(2)}, u32[]{:S(2)}) collective-permute-start(bf16[2,1024,64]{1,2,0:T(8,128)(2,1)S(1)} %pad_maximum_fusion.1), channel_id=1, source_target_pairs={{0,1016},{8,0},{16,8},{24,16},{32,24},{40,32},{48,40},{56,48},{64,... | collective-permute-start | bytes 786440 | tf_op jit(solution)/shard_map/ppermute | solution.py:14
  301.1 27.1 %all-to-all-start.8 = ((bf16[8,128,64]{1,2,0:T(8,128)(2,1)}), bf16[8,128,64]{1,2,0:T(8,128)(2,1)S(1)}, u32[]{:S(2)}, u32[]{:S(2)}) async-start(bf16[8,128,64]{1,2,0:T(8,128)(2,1)} %copy.74), calls=%async_computation.8 | async-start | bytes 262144 | tf_op jit(solution)/shard_map/all_to_all | solution.py:104
  328.2 27.2 %all-to-all-start.7 = ((bf16[8,128,64]{1,2,0:T(8,128)(2,1)}), bf16[8,128,64]{1,2,0:T(8,128)(2,1)S(1)}, u32[]{:S(2)}, u32[]{:S(2)}) async-start(bf16[8,128,64]{1,2,0:T(8,128)(2,1)} %copy.73), calls=%async_computation.7 | async-start | bytes 262144 | tf_op jit(solution)/shard_map/all_to_all | solution.py:103
  355.4 57.3 %all-to-all-start.6 = ((bf16[8,128,256]{2,1,0:T(8,128)(2,1)}), bf16[8,128,256]{2,1,0:T(8,128)(2,1)S(1)}, u32[]{:S(2)}, u32[]{:S(2)}) async-start(bf16[8,128,256]{2,1,0:T(8,128)(2,1)} %copy.71), calls=%async_computation.6 | async-start | bytes 1048576 | tf_op jit(solution)/shard_map/all_to_all | solution.py:102
where the time goes:
time: 415 us; the launch traced here: 414 us
  waiting for transfers between devices  270 us (65%)
  starting transfers between devices  82.1 us (20%)
  local copies, waits for them, and re-layouts  30.8 us (7%)
  matrix products  20.1 us (5%)
  loops' own time  7.97 us (2%)
    all_to_all x1, waiting for transfers between devices, per_device(): lax.all_to_all(grad_out, 'ulysses', split_axis=1, concat_axis=0, tiled=True)  59.2 us
    all_to_all x1, waiting for transfers between devices, per_device(): lax.all_to_all(grad_query, 'ulysses', split_axis=0, concat_axis=1, tiled=...  51.1 us
    all_to_all x1, starting transfers between devices, per_device(): lax.all_to_all(log_sums, 'ulysses', split_axis=1, concat_axis=0, tiled=True)  29.8 us
    all_to_all x1, waiting for transfers between devices, per_device(): lax.all_to_all(queries, 'ulysses', split_axis=1, concat_axis=0, tiled=True)  25.4 us
    all_to_all x1, waiting for transfers between devices, per_device(): lax.all_to_all(value_back, 'ulysses', split_axis=0, concat_axis=1, tiled=...  23 us
    all_to_all x1, waiting for transfers between devices, per_device(): lax.all_to_all(key_back, 'ulysses', split_axis=0, concat_axis=1, tiled=True)  22.6 us
    all_to_all x1, waiting for transfers between devices, per_device(): lax.all_to_all(delta, 'ulysses', split_axis=1, concat_axis=0, tiled=True)  22.2 us
    all_to_all x1, waiting for transfers between devices, per_device(): lax.all_to_all(key_states, 'ulysses', split_axis=1, concat_axis=0, tiled=...  22 us
  transfers between devices with their start and end apart: 11, of which 10 were waited for; matrix products, arithmetic and copies ran while one was open for 7% of the time, Pallas kernels for 0%

commit v1 on v0

v1 whole, which is shorter than its diff:
```python
import functools
import math

import jax
import jax.numpy as jnp
from jax import lax
from jax.experimental import pallas as pl
from jax.experimental.pallas import tpu as pltpu
from jax.sharding import PartitionSpec as P

HEAD_DIM = 64
LANES = 128
TOK = 128
RING = 4
HALF = TOK * RING
HEADS_LOCAL = 8
PAIRS = HEADS_LOCAL // 2
WIDTH = HEADS_LOCAL * HEAD_DIM
CROSS = 8
CROSS_ROWS = HALF // CROSS
AHEAD = 4
SLOTS = CROSS + AHEAD
LOCAL = 4
LOCAL_ROWS = HALF // LOCAL
PER_DEVICE = TOK // CROSS_ROWS
HIDE = 1e30
MESH = pl.DeviceIdType.MESH


def dot_nt(a, b):
    return lax.dot_general(a, b, (((1,), (1,)), ((), ())), preferred_element_type=jnp.float32)


def dot(a, b):
    return jnp.dot(a, b, preferred_element_type=jnp.float32)


def chunk_grads(key, value, sums_ref, delta_ref, query_ref, grad_ref, acc_ref):
    rows = key.shape[0]
    low = lax.broadcasted_iota(jnp.int32, (rows, LANES), 1) < HEAD_DIM
    zero = jnp.zeros((rows, LANES), jnp.float32)

    def spread(array, head):
        rolled = pltpu.roll(array, HEAD_DIM, 1)
        first, second = (array, rolled) if head == 0 else (rolled, array)
        return jnp.concatenate([jnp.where(low, first, zero), jnp.where(low, zero, second)], axis=0)

    def gather(first, second):
        one = first[:rows] + pltpu.roll(first[rows:], HEAD_DIM, 1)
        two = pltpu.roll(second[:rows], HEAD_DIM, 1) + second[rows:]
        return jnp.where(low, one, two)

    factor = 1.0 / math.sqrt(HEAD_DIM)
    key_f = key.astype(jnp.float32)
    value_f = value.astype(jnp.float32) * factor
    key_sums, value_sums = [], []
    for head in range(2):
        key_wide = spread(key_f, head)
        key_turned = key_wide.T.astype(jnp.bfloat16)
        key_wide = (key_wide * factor).astype(jnp.bfloat16)
        value_wide = spread(value_f, head).astype(jnp.bfloat16)
        key_sum, value_sum = None, None
        for pair in (2 * head, 2 * head + 1):
            cols = pl.ds(pair * LANES, LANES)
            query, grad = query_ref[:, cols], grad_ref[:, cols]
            scores = dot_nt(key_wide, query)
            dprobs = dot_nt(value_wide, grad)
            probs_b, dscores = [], []
            for one in range(2):
                part = slice(one * rows, (one + 1) * rows)
                at = pl.ds(2 * pair + one, 1)
                probs = jnp.exp(scores[part] - sums_ref[at, :])
                probs_b.append(probs.astype(jnp.bfloat16))
                dscores.append((probs * (dprobs[part] - delta_ref[at, :])).astype(jnp.bfloat16))
            probs_b = jnp.concatenate(probs_b, axis=0)
            dscores = jnp.concatenate(dscores, axis=0)
            value_piece, key_piece = dot(probs_b, grad), dot(dscores, query)
            value_sum = value_piece if value_sum is None else value_sum + value_piece
            key_sum = key_piece if key_sum is None else key_sum + key_piece
            acc_ref[cols, :] += dot(key_turned, dscores)
        key_sums.append(key_sum)
        value_sums.append(value_sum)
    return (gather(*key_sums), gather(*value_sums))


def kernel(
    n_blk,
    query_in,
    grad_in,
    key_in,
    value_in,
    stats_in,
    marks,
    query_out,
    both_out,
    query_g,
    grad_g,
    both_g,
    stats_g,
    sums_hid,
    acc,
    kept,
    slots,
    staged,
    query_s,
    both_s,
    wide_send,
    wide_recv,
    both_send,
    both_recv,
    slot_send,
    slot_recv,
    back_send,
    back_recv,
    out_send,
    out_recv,
    own_sem,
):
    blk, lane = lax.axis_index("blk"), lax.axis_index("ulysses")
    x, side = lax.rem(lane, RING), lane // RING
    after, before = lax.rem(blk + 1, n_blk), lax.rem(blk + n_blk - 1, n_blk)
    across = (blk, (1 - side) * RING + x)

    def peer(step):
        return lax.rem(x + step, RING)

    def at_x(block, where):
        return (block, side * RING + where)

    def remote(src, dst, send, recv, device):
        return pltpu.make_async_remote_copy(
            src_ref=src, dst_ref=dst, send_sem=send, recv_sem=recv, device_id=device, device_id_type=MESH
        )

    barrier = pltpu.get_barrier_semaphore()
    friends = [across] + [at_x(blk, peer(step)) for step in range(1, RING)]
    friends += [at_x(block, peer(step)) for block in (after, before) for step in range(RING)]
    for friend in friends:
        pl.semaphore_signal(barrier, inc=1, device_id=friend, device_id_type=MESH)
    acc[...] = jnp.zeros_like(acc)
    pl.semaphore_wait(barrier, len(friends))

    def rows_of(where):
        return pl.ds(pl.multiple_of(where * TOK, TOK), TOK)

    mine = rows_of(x)

    def both_copy(step, which):
        to = peer(step)
        cols = pl.ds(pl.multiple_of(to * LANES, LANES), LANES)
        src = (key_in, value_in)[which].at[:, cols]
        return remote(
            src, both_g.at[which, mine], both_send.at[step, which], both_recv.at[step, which], at_x(after, to)
        )

    for step in range(RING):
        for which in range(2):
            both_copy(step, which).start()

    def wide_parts(to):
        cols = pl.ds(pl.multiple_of(to * WIDTH, LANES), WIDTH)
        heads = pl.ds(pl.multiple_of(to * HEADS_LOCAL, HEADS_LOCAL), HEADS_LOCAL)
        lanes = pl.ds(pl.multiple_of(x * TOK, LANES), TOK)
        return (
            (query_in.at[:, cols], query_g.at[mine]),
            (grad_in.at[:, cols], grad_g.at[mine]),
            (stats_in.at[:, heads], stats_g.at[:, :, lanes]),
        )

    def wide_copy(step, which):
        src, dst = wide_parts(peer(step))[which]
        return remote(
            src, dst, wide_send.at[step - 1, which], wide_recv.at[step - 1, which], at_x(blk, peer(step))
        )

    for which in (2, 0, 1):
        for step in range(1, RING):
            wide_copy(step, which).start()
    own = [pltpu.make_async_copy(src, dst, own_sem.at[i]) for i, (src, dst) in enumerate(wide_parts(x))]
    for copy in own:
        copy.start()

    for step in range(RING):
        for which in range(2):
            both_copy(step, which).wait_recv()

    def chunk_rows(t, rows):
        return pl.ds(pl.multiple_of(t * rows, rows), rows)

    def first_copy(t):
        src = both_g.at[:, chunk_rows(t, CROSS_ROWS)]
        return remote(src, slots.at[t], slot_send.at[t], slot_recv.at[t], across)

    def later_copy(t):
        return remote(staged.at[t], slots.at[t + AHEAD], slot_send.at[t + AHEAD], slot_recv.at[t + AHEAD], across)

    for t in range(AHEAD):
        first_copy(t).start()

    for copy in own:
        copy.wait()
    for which in (2, 0, 1):
        for step in range(1, RING):
            wide_copy(step, which).wait_recv()

    for i in range(2):
        sums_hid[i] = stats_g[0] + jnp.concatenate([marks[i]] * RING, axis=1)

    grads = functools.partial(
        chunk_grads, delta_ref=stats_g.at[1], query_ref=query_g, grad_ref=grad_g, acc_ref=acc
    )

    def local_step(t, carry):
        rows = chunk_rows(t, LOCAL_ROWS)
        kept[0, rows], kept[1, rows] = grads(both_g[0, rows], both_g[1, rows], sums_hid.at[0])
        return carry

    lax.fori_loop(0, LOCAL, local_step, 0)

    gives = jnp.broadcast_to(marks[2, 0:1, :], (CROSS_ROWS, LANES)) > 0.5

    def slot_copy(t):
        return remote(slots.at[t], slots.at[t], slot_send.at[t], slot_recv.at[t], across)

    def out_copy(t):
        part = lax.rem(t, PER_DEVICE)
        rows = chunk_rows(part, CROSS_ROWS)
        cols = pl.ds(pl.multiple_of(x * LANES, LANES), LANES)
        return remote(
            both_s.at[t],
            both_out.at[:, rows, cols],
            out_send.at[t],
            out_recv.at[x, part],
            at_x(before, t // PER_DEVICE),
        )

    def finish(t):
        rows = chunk_rows(t, CROSS_ROWS)
        for which in range(2):
            came = jnp.where(gives, slots[t + AHEAD, which].astype(jnp.float32), 0.0)
            both_s[t, which] = (kept[which, rows] + came).astype(jnp.bfloat16)
        out_copy(t).start()

    def cross_step(t, carry):
        slot_copy(t).wait_recv()
        far = [jnp.where(gives, 0.0, slots[t, which].astype(jnp.float32)) for which in range(2)]
        out = grads(far[0], far[1], sums_hid.at[1])
        rows = chunk_rows(jnp.minimum(t + AHEAD, CROSS - 1), CROSS_ROWS)
        for which in range(2):
            given = both_g[which, rows].astype(jnp.float32)
            staged[t, which] = jnp.where(gives, given, out[which]).astype(jnp.bfloat16)
        later_copy(t).start()

        @pl.when(t >= AHEAD)
        def _():
            finish(t - AHEAD)

        return carry

    lax.fori_loop(0, CROSS, cross_step, 0)

    def back_copy(step):
        cols = pl.ds(pl.multiple_of(x * WIDTH, LANES), WIDTH)
        return remote(
            query_s.at[step],
            query_out.at[:, cols],
            back_send.at[step - 1],
            back_recv.at[step - 1],
            at_x(blk, peer(step)),
        )

    for step in (1, 2, 3, 0):
        lanes = pl.ds(pl.multiple_of(peer(step) * TOK, LANES), TOK)
        turned = acc[:, lanes].T.astype(jnp.bfloat16)
        if step == 0:
            query_out[:, pl.ds(pl.multiple_of(x * WIDTH, LANES), WIDTH)] = turned
        else:
            query_s[step] = turned
            back_copy(step).start()

    def last_step(t, carry):
        slot_copy(t).wait_recv()
        finish(t - AHEAD)
        return carry

    lax.fori_loop(CROSS, SLOTS, last_step, 0)

    for step in range(1, RING):
        back_copy(step).wait_recv()

    def arrived(i, carry):
        where, part = i // PER_DEVICE, lax.rem(i, PER_DEVICE)
        cols = pl.ds(pl.multiple_of(where * LANES, LANES), LANES)
        dst = both_out.at[:, chunk_rows(part, CROSS_ROWS), cols]
        remote(both_s.at[0], dst, out_send.at[0], out_recv.at[where, part], across).wait_recv()
        return carry

    lax.fori_loop(0, RING * PER_DEVICE, arrived, 0)

    for step in range(RING):
        for which in range(2):
            both_copy(step, which).wait_send()
    for step in range(1, RING):
        for which in range(3):
            wide_copy(step, which).wait_send()
        back_copy(step).wait_send()
    for t in range(AHEAD):
        first_copy(t).wait_send()
    for t in range(CROSS):
        later_copy(t).wait_send()
        out_copy(t).wait_send()


def per_device(n_blk, queries, key_states, value_states, attn_out, grad_out, log_sums, owners):
    heads = log_sums.shape[1]
    wide = jnp.float32
    delta = jnp.sum((grad_out.astype(wide) * attn_out.astype(wide)).reshape(TOK, heads, HEAD_DIM), axis=2)
    stats = jnp.stack([log_sums.T, delta.T * (1.0 / math.sqrt(HEAD_DIM))])
    blk, side = lax.axis_index("blk"), lax.axis_index("ulysses") // RING
    before = (blk + n_blk - 1) % n_blk
    query_half = owners[2 * blk + side]
    sees_near = query_half > owners[2 * before + side]
    sees_far = query_half > owners[2 * before + 1 - side]
    marks = jnp.stack(
        [jnp.where(sees_near, 0.0, HIDE), jnp.where(sees_far, 0.0, HIDE), jnp.where(sees_far, 0.0, 1.0)]
    ).astype(wide)
    marks = jnp.broadcast_to(marks[:, None, None], (3, HEADS_LOCAL, LANES))
    hbm, vmem = pl.BlockSpec(memory_space=pl.ANY), pl.BlockSpec(memory_space=pltpu.VMEM)
    narrow = jnp.bfloat16
    dma = pltpu.SemaphoreType.DMA
    grad_query, both = pl.pallas_call(
        functools.partial(kernel, n_blk),
        out_shape=(
            jax.ShapeDtypeStruct((TOK, heads * HEAD_DIM), narrow),
            jax.ShapeDtypeStruct((2, TOK, RING * LANES), narrow),
        ),
        in_specs=[hbm, hbm, hbm, hbm, vmem, vmem],
        out_specs=(vmem, vmem),
        scratch_shapes=[
            pltpu.VMEM((HALF, WIDTH), narrow),
            pltpu.VMEM((HALF, WIDTH), narrow),
            pltpu.VMEM((2, HALF, LANES), narrow),
            pltpu.VMEM((2, HEADS_LOCAL, HALF), wide),
            pltpu.VMEM((2, HEADS_LOCAL, HALF), wide),
            pltpu.VMEM((WIDTH, HALF), wide),
            pltpu.VMEM((2, HALF, LANES), wide),
            pltpu.VMEM((SLOTS, 2, CROSS_ROWS, LANES), narrow),
            pltpu.VMEM((CROSS, 2, CROSS_ROWS, LANES), narrow),
            pltpu.VMEM((RING, TOK, WIDTH), narrow),
            pltpu.VMEM((CROSS, 2, CROSS_ROWS, LANES), narrow),
            dma((RING - 1, 3)),
            dma((RING - 1, 3)),
            dma((RING, 2)),
            dma((RING, 2)),
            dma((SLOTS,)),
            dma((SLOTS,)),
            dma((RING - 1,)),
            dma((RING - 1,)),
            dma((CROSS,)),
            dma((RING, PER_DEVICE)),
            dma((3,)),
        ],
        compiler_params=pltpu.CompilerParams(
            collective_id=0, has_side_effects=True, vmem_limit_bytes=48 * 1024 * 1024
        ),
    )(queries, grad_out, key_states, value_states, stats, marks)
    return (grad_query, both[0], both[1])


def solution(mesh):
    rows = P(("blk", "ulysses"), None)
    return jax.shard_map(
        functools.partial(per_device, mesh.shape["blk"]),
        mesh=mesh,
        in_specs=(rows, rows, rows, rows, rows, rows, P(None)),
        out_specs=(rows, rows, rows),
        check_vma=False,
    )
```

time: 415 us -> 141 us (0.34)
  the two profiles are of different devices: /device:TPU:57 before, /device:TPU:7 now
where the time goes in v1:
time: 141 us; the launch traced here: 140 us
  Pallas kernels  131 us (93%)
  local copies, waits for them, and re-layouts  5.33 us (4%)
  between operations  3.36 us (2%)
    pallas_call x1, Pallas kernels, per_device(): pl.pallas_call(functools.partial(kernel, n_blk), out_shape=(jax.ShapeDtyp...  131 us
    unnamed x15, local copies, waits for them, and re-layouts  3.95 us

profile of v1, /device:TPU:7, one launch (start us, length us, event | category | flops | bytes accessed | tf_op | source)
XLA Modules:
  0.0 140.3 jit_solution(10407945683760346974)
XLA Ops:
  0.7 0.0 copy-start.5
  0.7 0.7 copy-done.5
  1.4 0.6 fusion
  4.5 0.1 pad_maximum_fusion.1
  4.6 0.1 broadcast_in_dim.2.marks
  4.7 0.0 copy-start
  4.7 1.4 copy.11
  6.1 0.0 copy-done
  6.1 0.3 copy.10
  6.4 0.0 copy-start.1
  6.4 0.0 copy-start.2
  6.4 0.0 copy-start.3
  6.4 0.2 bitcast_reduce_fusion
  6.6 0.0 copy-start.4
  6.6 0.7 copy-done.4
  7.3 0.1 copy-done.1
  7.4 0.0 copy-done.2
  7.4 0.0 copy-done.3
  7.5 131.3 %shard_map.94 = (bf16[128,2048]{1,0:T(8,128)(2,1)S(1)}, bf16[2,128,512]{2,1,0:T(8,128)(2,1)S(1)}) custom-call(bf16[128,2048]{1,0:T(8,128)(2,1)S(1)} %copy-done.1, bf16[128,2048]{1,0:T(8,128)(2,1)S(1)} %copy-done, bf16[128,512]{1,0:T(8,128)(2,1)S(1)} %copy-done.2, bf16[128,512]{1,0:T(8,128)(2,1)S(1)} %copy-done.3, ...), custom_call_target="tpu_custom_call" | custom-call | tf_op jit(solution)/shard_map/pallas_call | solution.py:331
  138.7 0.7 slice_bitcast_fusion
  139.5 0.8 copy.13
  (2 shorter events, 0.0 us)
Async XLA Ops:
  0.7 0.7 copy-start.5
  4.7 1.4 copy-start
  6.4 1.0 copy-start.1
  6.4 1.1 copy-start.2
  6.4 1.1 copy-start.3
  6.6 0.7 copy-start.4

commit v2 on v1

--- a/solution.py
+++ b/solution.py
@@ -16,13 +16,12 @@
 HEADS_LOCAL = 8
 PAIRS = HEADS_LOCAL // 2
 WIDTH = HEADS_LOCAL * HEAD_DIM
-CROSS = 8
+CROSS = 16
 CROSS_ROWS = HALF // CROSS
-AHEAD = 4
+AHEAD = 5
 SLOTS = CROSS + AHEAD
-LOCAL = 4
-LOCAL_ROWS = HALF // LOCAL
 PER_DEVICE = TOK // CROSS_ROWS
+TURN = 32
 HIDE = 1e30
 MESH = pl.DeviceIdType.MESH
 
@@ -89,10 +88,14 @@
     grad_in,
     key_in,
     value_in,
-    stats_in,
-    marks,
+    out_in,
+    sums_in,
+    owners,
     query_out,
     both_out,
+    grad_v,
+    out_v,
+    stats_in,
     query_g,
     grad_g,
     both_g,
@@ -115,17 +118,25 @@
     out_send,
     out_recv,
     own_sem,
+    load_sem,
 ):
     blk, lane = lax.axis_index("blk"), lax.axis_index("ulysses")
     x, side = lax.rem(lane, RING), lane // RING
     after, before = lax.rem(blk + 1, n_blk), lax.rem(blk + n_blk - 1, n_blk)
     across = (blk, (1 - side) * RING + x)
 
+    def turned(block):
+        wraps = jnp.where(lax.rem(block, TURN) == 0, 1, 0)
+        return lax.rem(side + wraps, 2)
+
+    near = {"after": (after, turned(after)), "before": (before, turned(blk)), "same": (blk, side)}
+
     def peer(step):
         return lax.rem(x + step, RING)
 
-    def at_x(block, where):
-        return (block, side * RING + where)
+    def at_x(name, where):
+        block, half = near[name]
+        return (block, half * RING + where)
 
     def remote(src, dst, send, recv, device):
         return pltpu.make_async_remote_copy(
@@ -133,11 +144,32 @@
         )
 
     barrier = pltpu.get_barrier_semaphore()
-    friends = [across] + [at_x(blk, peer(step)) for step in range(1, RING)]
-    friends += [at_x(block, peer(step)) for block in (after, before) for step in range(RING)]
+    friends = [across] + [at_x("same", peer(step)) for step in range(1, RING)]
+    friends += [at_x(name, peer(step)) for name in ("after", "before") for step in range(RING)]
     for friend in friends:
         pl.semaphore_signal(barrier, inc=1, device_id=friend, device_id_type=MESH)
+
+    loads = [
+        pltpu.make_async_copy(src, dst, load_sem.at[i])
+        for i, (src, dst) in enumerate(((grad_in, grad_v), (out_in, out_v), (sums_in, stats_in.at[0])))
+    ]
+    for copy in loads:
+        copy.start()
     acc[...] = jnp.zeros_like(acc)
+    query_half = jnp.full((HEADS_LOCAL, LANES), owners[2 * blk + side], jnp.int32)
+    near_half = jnp.full((HEADS_LOCAL, LANES), owners[2 * before + near["before"][1]], jnp.int32)
+    far_half = jnp.full((HEADS_LOCAL, LANES), owners[2 * before + 1 - near["before"][1]], jnp.int32)
+    marks = [jnp.where(query_half > other, 0.0, HIDE) for other in (near_half, far_half)]
+    for copy in loads:
+        copy.wait()
+    factor = 1.0 / math.sqrt(HEAD_DIM)
+    for i in range(grad_v.shape[1] // LANES):
+        cols = pl.ds(i * LANES, LANES)
+        product = (grad_v[:, cols].astype(jnp.float32) * out_v[:, cols].astype(jnp.float32)).T
+        for one in range(2):
+            total = jnp.sum(product[one * HEAD_DIM : (one + 1) * HEAD_DIM], axis=0, keepdims=True)
+            stats_in[1, pl.ds(2 * i + one, 1), :] = total * factor
+
     pl.semaphore_wait(barrier, len(friends))
 
     def rows_of(where):
@@ -150,7 +182,7 @@
         cols = pl.ds(pl.multiple_of(to * LANES, LANES), LANES)
         src = (key_in, value_in)[which].at[:, cols]
         return remote(
-            src, both_g.at[which, mine], both_send.at[step, which], both_recv.at[step, which], at_x(after, to)
+            src, both_g.at[which, mine], both_send.at[step, which], both_recv.at[step, which], at_x("after", to)
         )
 
     for step in range(RING):
@@ -170,7 +202,7 @@
     def wide_copy(step, which):
         src, dst = wide_parts(peer(step))[which]
         return remote(
-            src, dst, wide_send.at[step - 1, which], wide_recv.at[step - 1, which], at_x(blk, peer(step))
+            src, dst, wide_send.at[step - 1, which], wide_recv.at[step - 1, which], at_x("same", peer(step))
         )
 
     for which in (2, 0, 1):
@@ -210,14 +242,7 @@
         chunk_grads, delta_ref=stats_g.at[1], query_ref=query_g, grad_ref=grad_g, acc_ref=acc
     )
 
-    def local_step(t, carry):
-        rows = chunk_rows(t, LOCAL_ROWS)
-        kept[0, rows], kept[1, rows] = grads(both_g[0, rows], both_g[1, rows], sums_hid.at[0])
-        return carry
-
-    lax.fori_loop(0, LOCAL, local_step, 0)
-
-    gives = jnp.broadcast_to(marks[2, 0:1, :], (CROSS_ROWS, LANES)) > 0.5
+    gives = jnp.broadcast_to(marks[1][0:1, :], (CROSS_ROWS, LANES)) > 0.5
 
     def slot_copy(t):
         return remote(slots.at[t], slots.at[t], slot_send.at[t], slot_recv.at[t], across)
@@ -231,7 +256,7 @@
             both_out.at[:, rows, cols],
             out_send.at[t],
             out_recv.at[x, part],
-            at_x(before, t // PER_DEVICE),
+            at_x("before", t // PER_DEVICE),
         )
 
     def finish(t):
@@ -250,6 +275,8 @@
             given = both_g[which, rows].astype(jnp.float32)
             staged[t, which] = jnp.where(gives, given, out[which]).astype(jnp.bfloat16)
         later_copy(t).start()
+        rows = chunk_rows(t, CROSS_ROWS)
+        kept[0, rows], kept[1, rows] = grads(both_g[0, rows], both_g[1, rows], sums_hid.at[0])
 
         @pl.when(t >= AHEAD)
         def _():
@@ -266,7 +293,7 @@
             query_out.at[:, cols],
             back_send.at[step - 1],
             back_recv.at[step - 1],
-            at_x(blk, peer(step)),
+            at_x("same", peer(step)),
         )
 
     for step in (1, 2, 3, 0):
@@ -312,20 +339,9 @@
 
 
 def per_device(n_blk, queries, key_states, value_states, attn_out, grad_out, log_sums, owners):
-    heads = log_sums.shape[1]
-    wide = jnp.float32
-    delta = jnp.sum((grad_out.astype(wide) * attn_out.astype(wide)).reshape(TOK, heads, HEAD_DIM), axis=2)
-    stats = jnp.stack([log_sums.T, delta.T * (1.0 / math.sqrt(HEAD_DIM))])
-    blk, side = lax.axis_index("blk"), lax.axis_index("ulysses") // RING
-    before = (blk + n_blk - 1) % n_blk
-    query_half = owners[2 * blk + side]
-    sees_near = query_half > owners[2 * before + side]
-    sees_far = query_half > owners[2 * before + 1 - side]
-    marks = jnp.stack(
-        [jnp.where(sees_near, 0.0, HIDE), jnp.where(sees_far, 0.0, HIDE), jnp.where(sees_far, 0.0, 1.0)]
-    ).astype(wide)
-    marks = jnp.broadcast_to(marks[:, None, None], (3, HEADS_LOCAL, LANES))
-    hbm, vmem = pl.BlockSpec(memory_space=pl.ANY), pl.BlockSpec(memory_space=pltpu.VMEM)
+    heads, wide = log_sums.shape[1], jnp.float32
+    hbm, vmem = pl.BlockSpec(memory_space=pltpu.HBM), pl.BlockSpec(memory_space=pltpu.VMEM)
+    smem = pl.BlockSpec(memory_space=pltpu.SMEM)
     narrow = jnp.bfloat16
     dma = pltpu.SemaphoreType.DMA
     grad_query, both = pl.pallas_call(
@@ -334,9 +350,12 @@
             jax.ShapeDtypeStruct((TOK, heads * HEAD_DIM), narrow),
             jax.ShapeDtypeStruct((2, TOK, RING * LANES), narrow),
         ),
-        in_specs=[hbm, hbm, hbm, hbm, vmem, vmem],
+        in_specs=[hbm, hbm, hbm, hbm, hbm, hbm, smem],
         out_specs=(vmem, vmem),
         scratch_shapes=[
+            pltpu.VMEM((TOK, heads * HEAD_DIM), narrow),
+            pltpu.VMEM((TOK, heads * HEAD_DIM), narrow),
+            pltpu.VMEM((2, heads, TOK), wide),
             pltpu.VMEM((HALF, WIDTH), narrow),
             pltpu.VMEM((HALF, WIDTH), narrow),
             pltpu.VMEM((2, HALF, LANES), narrow),
@@ -359,11 +378,12 @@
             dma((CROSS,)),
             dma((RING, PER_DEVICE)),
             dma((3,)),
+            dma((3,)),
         ],
         compiler_params=pltpu.CompilerParams(
-            collective_id=0, has_side_effects=True, vmem_limit_bytes=48 * 1024 * 1024
+            collective_id=0, has_side_effects=True, vmem_limit_bytes=67043328
         ),
-    )(queries, grad_out, key_states, value_states, stats, marks)
+    )(queries, grad_out, key_states, value_states, attn_out, log_sums.T, owners)
     return (grad_query, both[0], both[1])
 
 

time: 141 us -> 130 us (0.922)
  the two profiles are of different devices: /device:TPU:7 before, /device:TPU:6 now
where the time goes in v2:
time: 130 us
  Pallas kernels  126 us (97%)
  local copies, waits for them, and re-layouts  2.54 us (2%)
    pallas_call x1, Pallas kernels, per_device(): pl.pallas_call(functools.partial(kernel, n_blk), out_shape=(jax.ShapeDtyp...  126 us

profile of v2, /device:TPU:6, one launch (start us, length us, event | category | flops | bytes accessed | tf_op | source)
XLA Modules:
  0.0 129.7 jit_solution(12639540679825515144)
XLA Ops:
  0.6 126.5 %shard_map.94 = (bf16[128,2048]{1,0:T(8,128)(2,1)}, bf16[2,128,512]{2,1,0:T(8,128)(2,1)}) custom-call(bf16[128,2048]{1,0:T(8,128)(2,1)} %query_in.1, bf16[128,2048]{1,0:T(8,128)(2,1)} %grad_in.1, bf16[128,512]{1,0:T(8,128)(2,1)} %key_in.1, bf16[128,512]{1,0:T(8,128)(2,1)} %value_in.1, bf16[128,2048]{1,0:T(8,128)(2,1)} %out_in.1, f32[32,128]{1,0:T(8,128)} %bitcast.5, ...), custom_call_target="tpu_custom_call" | custom-call | tf_op jit(solution)/shard_map/pallas_call | solution.py:347
  127.1 0.0 copy-start
  127.1 1.7 %slice_bitcast_fusion = (bf16[128,512]{1,0:T(8,128)(2,1)}, bf16[128,512]{1,0:T(8,128)(2,1)}) fusion(bf16[2,128,512]{2,1,0:T(8,128)(2,1)} %get-tuple-element.6), kind=kLoop, calls=%fused_computation | loop fusion | bytes 524288 | tf_op jit(solution)/shard_map/squeeze | solution.py:387
  128.9 0.0 copy-done
  128.9 0.8 copy.11
Async XLA Ops:
  127.1 1.8 %copy-start = (bf16[128,2048]{1,0:T(8,128)(2,1)S(1)}, bf16[128,2048]{1,0:T(8,128)(2,1)}, u32[]{:S(2)}) copy-start(bf16[128,2048]{1,0:T(8,128)(2,1)} %get-tuple-element.12) | copy-start | bytes 1572868

commit v3 on v2

--- a/solution.py
+++ b/solution.py
@@ -20,8 +20,11 @@
 CROSS_ROWS = HALF // CROSS
 AHEAD = 5
 SLOTS = CROSS + AHEAD
+NEAR_ROWS = 128
+EARLY = 2
 PER_DEVICE = TOK // CROSS_ROWS
 TURN = 32
+LEGS = 4
 HIDE = 1e30
 MESH = pl.DeviceIdType.MESH
 
@@ -119,6 +122,7 @@
     out_recv,
     own_sem,
     load_sem,
+    word_sem,
 ):
     blk, lane = lax.axis_index("blk"), lax.axis_index("ulysses")
     x, side = lax.rem(lane, RING), lane // RING
@@ -131,6 +135,14 @@
 
     near = {"after": (after, turned(after)), "before": (before, turned(blk)), "same": (blk, side)}
 
+    def along(steps):
+        row = TURN // 2
+        spot = lax.rem(side * row + lax.rem(blk, TURN) // 2 + steps + 2 * row, 2 * row)
+        there = (blk // TURN) * TURN + lax.rem(spot, row) * 2 + lax.rem(blk, 2)
+        return (there, (spot // row) * RING + x)
+
+    leg = TURN // 2 // LEGS
+
     def peer(step):
         return lax.rem(x + step, RING)
 
@@ -144,7 +156,7 @@
         )
 
     barrier = pltpu.get_barrier_semaphore()
-    friends = [across] + [at_x("same", peer(step)) for step in range(1, RING)]
+    friends = [along(leg), along(-leg)] + [at_x("same", peer(step)) for step in range(1, RING)]
     friends += [at_x(name, peer(step)) for name in ("after", "before") for step in range(RING)]
     for friend in friends:
         pl.semaphore_signal(barrier, inc=1, device_id=friend, device_id_type=MESH)
@@ -155,6 +167,49 @@
     ]
     for copy in loads:
         copy.start()
+    pl.semaphore_wait(barrier, len(friends))
+
+    def rows_of(where):
+        return pl.ds(pl.multiple_of(where * TOK, TOK), TOK)
+
+    mine = rows_of(x)
+
+    def both_copy(step, which):
+        to = peer(step)
+        cols = pl.ds(pl.multiple_of(to * LANES, LANES), LANES)
+        src = (key_in, value_in)[which].at[:, cols]
+        return remote(
+            src, both_g.at[which, mine], both_send.at[step, which], both_recv.at[step, which], at_x("after", to)
+        )
+
+    for step in range(RING):
+        for which in range(2):
+            both_copy(step, which).start()
+
+    def wide_parts(to):
+        cols = pl.ds(pl.multiple_of(to * WIDTH, LANES), WIDTH)
+        heads = pl.ds(pl.multiple_of(to * HEADS_LOCAL, HEADS_LOCAL), HEADS_LOCAL)
+        lanes = pl.ds(pl.multiple_of(x * TOK, LANES), TOK)
+        return (
+            (query_in.at[:, cols], query_g.at[mine]),
+            (grad_in.at[:, cols], grad_g.at[mine]),
+            (stats_in.at[:, heads], stats_g.at[:, :, lanes]),
+        )
+
+    def wide_copy(step, which):
+        src, dst = wide_parts(peer(step))[which]
+        return remote(
+            src, dst, wide_send.at[step - 1, which], wide_recv.at[step - 1, which], at_x("same", peer(step))
+        )
+
+    for which in (0, 1):
+        for step in range(1, RING):
+            wide_copy(step, which).start()
+
+    def pass_word(stop):
+        pl.semaphore_signal(word_sem.at[stop], inc=1, device_id=along(-leg), device_id_type=MESH)
+
+    pass_word(0)
     acc[...] = jnp.zeros_like(acc)
     query_half = jnp.full((HEADS_LOCAL, LANES), owners[2 * blk + side], jnp.int32)
     near_half = jnp.full((HEADS_LOCAL, LANES), owners[2 * before + near["before"][1]], jnp.int32)
@@ -170,44 +225,11 @@
             total = jnp.sum(product[one * HEAD_DIM : (one + 1) * HEAD_DIM], axis=0, keepdims=True)
             stats_in[1, pl.ds(2 * i + one, 1), :] = total * factor
 
-    pl.semaphore_wait(barrier, len(friends))
-
-    def rows_of(where):
-        return pl.ds(pl.multiple_of(where * TOK, TOK), TOK)
-
-    mine = rows_of(x)
-
-    def both_copy(step, which):
-        to = peer(step)
-        cols = pl.ds(pl.multiple_of(to * LANES, LANES), LANES)
-        src = (key_in, value_in)[which].at[:, cols]
-        return remote(
-            src, both_g.at[which, mine], both_send.at[step, which], both_recv.at[step, which], at_x("after", to)
-        )
-
-    for step in range(RING):
-        for which in range(2):
-            both_copy(step, which).start()
-
-    def wide_parts(to):
-        cols = pl.ds(pl.multiple_of(to * WIDTH, LANES), WIDTH)
-        heads = pl.ds(pl.multiple_of(to * HEADS_LOCAL, HEADS_LOCAL), HEADS_LOCAL)
-        lanes = pl.ds(pl.multiple_of(x * TOK, LANES), TOK)
-        return (
-            (query_in.at[:, cols], query_g.at[mine]),
-            (grad_in.at[:, cols], grad_g.at[mine]),
-            (stats_in.at[:, heads], stats_g.at[:, :, lanes]),
-        )
-
-    def wide_copy(step, which):
-        src, dst = wide_parts(peer(step))[which]
-        return remote(
-            src, dst, wide_send.at[step - 1, which], wide_recv.at[step - 1, which], at_x("same", peer(step))
-        )
-
-    for which in (2, 0, 1):
-        for step in range(1, RING):
-            wide_copy(step, which).start()
+    for stop in range(1, LEGS - 1):
+        pl.semaphore_wait(word_sem.at[stop - 1], 1)
+        pass_word(stop)
+    for step in range(1, RING):
+        wide_copy(step, 2).start()
     own = [pltpu.make_async_copy(src, dst, own_sem.at[i]) for i, (src, dst) in enumerate(wide_parts(x))]
     for copy in own:
         copy.start()
@@ -215,6 +237,7 @@
     for step in range(RING):
         for which in range(2):
             both_copy(step, which).wait_recv()
+    pl.semaphore_wait(word_sem.at[LEGS - 2], 1)
 
     def chunk_rows(t, rows):
         return pl.ds(pl.multiple_of(t * rows, rows), rows)
@@ -241,6 +264,14 @@
     grads = functools.partial(
         chunk_grads, delta_ref=stats_g.at[1], query_ref=query_g, grad_ref=grad_g, acc_ref=acc
     )
+
+    def near_step(t, carry):
+        rows = chunk_rows(t, NEAR_ROWS)
+        kept[0, rows], kept[1, rows] = grads(both_g[0, rows], both_g[1, rows], sums_hid.at[0])
+        return carry
+
+    lax.fori_loop(0, EARLY, near_step, 0)
+    ready = EARLY * NEAR_ROWS // CROSS_ROWS + AHEAD
 
     gives = jnp.broadcast_to(marks[1][0:1, :], (CROSS_ROWS, LANES)) > 0.5
 
@@ -275,16 +306,15 @@
             given = both_g[which, rows].astype(jnp.float32)
             staged[t, which] = jnp.where(gives, given, out[which]).astype(jnp.bfloat16)
         later_copy(t).start()
-        rows = chunk_rows(t, CROSS_ROWS)
-        kept[0, rows], kept[1, rows] = grads(both_g[0, rows], both_g[1, rows], sums_hid.at[0])
-
-        @pl.when(t >= AHEAD)
+
+        @pl.when((t >= AHEAD) & (t < ready))
         def _():
             finish(t - AHEAD)
 
         return carry
 
     lax.fori_loop(0, CROSS, cross_step, 0)
+    lax.fori_loop(EARLY, HALF // NEAR_ROWS, near_step, 0)
 
     def back_copy(step):
         cols = pl.ds(pl.multiple_of(x * WIDTH, LANES), WIDTH)
@@ -305,11 +335,16 @@
             query_s[step] = turned
             back_copy(step).start()
 
+    def late_step(t, carry):
+        finish(t - AHEAD)
+        return carry
+
     def last_step(t, carry):
         slot_copy(t).wait_recv()
         finish(t - AHEAD)
         return carry
 
+    lax.fori_loop(ready, CROSS, late_step, 0)
     lax.fori_loop(CROSS, SLOTS, last_step, 0)
 
     for step in range(1, RING):
@@ -379,6 +414,7 @@
             dma((RING, PER_DEVICE)),
             dma((3,)),
             dma((3,)),
+            pltpu.SemaphoreType.REGULAR((LEGS - 1,)),
         ],
         compiler_params=pltpu.CompilerParams(
             collective_id=0, has_side_effects=True, vmem_limit_bytes=67043328

time: 130 us -> 124 us (0.954)
  the two profiles are of different devices: /device:TPU:6 before, /device:TPU:39 now
where the time goes in v3:
time: 124 us; the launch traced here: 123 us
  Pallas kernels  120 us (97%)
  local copies, waits for them, and re-layouts  2.54 us (2%)
    pallas_call x1, Pallas kernels, per_device(): pl.pallas_call(functools.partial(kernel, n_blk), out_shape=(jax.ShapeDtyp...  120 us

profile of v3, /device:TPU:39, one launch (start us, length us, event | category | flops | bytes accessed | tf_op | source)
XLA Modules:
  0.0 123.4 jit_solution(12102173356859732171)
XLA Ops:
  0.6 120.2 %shard_map.94 = (bf16[128,2048]{1,0:T(8,128)(2,1)}, bf16[2,128,512]{2,1,0:T(8,128)(2,1)}) custom-call(bf16[128,2048]{1,0:T(8,128)(2,1)} %query_in.1, bf16[128,2048]{1,0:T(8,128)(2,1)} %grad_in.1, bf16[128,512]{1,0:T(8,128)(2,1)} %key_in.1, bf16[128,512]{1,0:T(8,128)(2,1)} %value_in.1, bf16[128,2048]{1,0:T(8,128)(2,1)} %out_in.1, f32[32,128]{1,0:T(8,128)} %bitcast.5, ...), custom_call_target="tpu_custom_call" | custom-call | tf_op jit(solution)/shard_map/pallas_call | solution.py:382
  120.8 0.0 copy-start
  120.8 1.7 %slice_bitcast_fusion = (bf16[128,512]{1,0:T(8,128)(2,1)}, bf16[128,512]{1,0:T(8,128)(2,1)}) fusion(bf16[2,128,512]{2,1,0:T(8,128)(2,1)} %get-tuple-element.6), kind=kLoop, calls=%fused_computation | loop fusion | bytes 524288 | tf_op jit(solution)/shard_map/squeeze | solution.py:423
  122.6 0.0 copy-done
  122.6 0.8 copy.11
Async XLA Ops:
  120.8 1.8 %copy-start = (bf16[128,2048]{1,0:T(8,128)(2,1)S(1)}, bf16[128,2048]{1,0:T(8,128)(2,1)}, u32[]{:S(2)}) copy-start(bf16[128,2048]{1,0:T(8,128)(2,1)} %get-tuple-element.12) | copy-start | bytes 1572868

commit v4 on v3

--- a/solution.py
+++ b/solution.py
@@ -37,7 +37,7 @@
     return jnp.dot(a, b, preferred_element_type=jnp.float32)
 
 
-def chunk_grads(key, value, sums_ref, delta_ref, query_ref, grad_ref, acc_ref):
+def chunk_grads(key, value, sums_ref, at_row, delta_ref, query_ref, grad_ref, keys_ref, dscores_ref):
     rows = key.shape[0]
     low = lax.broadcasted_iota(jnp.int32, (rows, LANES), 1) < HEAD_DIM
     zero = jnp.zeros((rows, LANES), jnp.float32)
@@ -58,7 +58,8 @@
     key_sums, value_sums = [], []
     for head in range(2):
         key_wide = spread(key_f, head)
-        key_turned = key_wide.T.astype(jnp.bfloat16)
+        kept_rows = pl.ds(pl.multiple_of(at_row, 2 * rows), 2 * rows)
+        keys_ref[head, kept_rows] = key_wide.astype(jnp.bfloat16)
         key_wide = (key_wide * factor).astype(jnp.bfloat16)
         value_wide = spread(value_f, head).astype(jnp.bfloat16)
         key_sum, value_sum = None, None
@@ -79,7 +80,7 @@
             value_piece, key_piece = dot(probs_b, grad), dot(dscores, query)
             value_sum = value_piece if value_sum is None else value_sum + value_piece
             key_sum = key_piece if key_sum is None else key_sum + key_piece
-            acc_ref[cols, :] += dot(key_turned, dscores)
+            dscores_ref[pair, kept_rows] = dscores
         key_sums.append(key_sum)
         value_sums.append(value_sum)
     return (gather(*key_sums), gather(*value_sums))
@@ -105,6 +106,8 @@
     stats_g,
     sums_hid,
     acc,
+    keys_s,
+    dscores_s,
     kept,
     slots,
     staged,
@@ -210,7 +213,6 @@
         pl.semaphore_signal(word_sem.at[stop], inc=1, device_id=along(-leg), device_id_type=MESH)
 
     pass_word(0)
-    acc[...] = jnp.zeros_like(acc)
     query_half = jnp.full((HEADS_LOCAL, LANES), owners[2 * blk + side], jnp.int32)
     near_half = jnp.full((HEADS_LOCAL, LANES), owners[2 * before + near["before"][1]], jnp.int32)
     far_half = jnp.full((HEADS_LOCAL, LANES), owners[2 * before + 1 - near["before"][1]], jnp.int32)
@@ -262,12 +264,12 @@
         sums_hid[i] = stats_g[0] + jnp.concatenate([marks[i]] * RING, axis=1)
 
     grads = functools.partial(
-        chunk_grads, delta_ref=stats_g.at[1], query_ref=query_g, grad_ref=grad_g, acc_ref=acc
+        chunk_grads, delta_ref=stats_g.at[1], query_ref=query_g, grad_ref=grad_g, keys_ref=keys_s, dscores_ref=dscores_s
     )
 
     def near_step(t, carry):
         rows = chunk_rows(t, NEAR_ROWS)
-        kept[0, rows], kept[1, rows] = grads(both_g[0, rows], both_g[1, rows], sums_hid.at[0])
+        kept[0, rows], kept[1, rows] = grads(both_g[0, rows], both_g[1, rows], sums_hid.at[0], t * (2 * NEAR_ROWS))
         return carry
 
     lax.fori_loop(0, EARLY, near_step, 0)
@@ -300,7 +302,7 @@
     def cross_step(t, carry):
         slot_copy(t).wait_recv()
         far = [jnp.where(gives, 0.0, slots[t, which].astype(jnp.float32)) for which in range(2)]
-        out = grads(far[0], far[1], sums_hid.at[1])
+        out = grads(far[0], far[1], sums_hid.at[1], 2 * HALF + t * (2 * CROSS_ROWS))
         rows = chunk_rows(jnp.minimum(t + AHEAD, CROSS - 1), CROSS_ROWS)
         for which in range(2):
             given = both_g[which, rows].astype(jnp.float32)
@@ -315,6 +317,11 @@
 
     lax.fori_loop(0, CROSS, cross_step, 0)
     lax.fori_loop(EARLY, HALF // NEAR_ROWS, near_step, 0)
+
+    for head in range(2):
+        keys_turned = keys_s[head].astype(jnp.float32).T.astype(jnp.bfloat16)
+        for pair in (2 * head, 2 * head + 1):
+            acc[pl.ds(pair * LANES, LANES), :] = dot(keys_turned, dscores_s[pair])
 
     def back_copy(step):
         cols = pl.ds(pl.multiple_of(x * WIDTH, LANES), WIDTH)
@@ -397,6 +404,8 @@
             pltpu.VMEM((2, HEADS_LOCAL, HALF), wide),
             pltpu.VMEM((2, HEADS_LOCAL, HALF), wide),
             pltpu.VMEM((WIDTH, HALF), wide),
+            pltpu.VMEM((2, 4 * HALF, LANES), narrow),
+            pltpu.VMEM((PAIRS, 4 * HALF, HALF), narrow),
             pltpu.VMEM((2, HALF, LANES), wide),
             pltpu.VMEM((SLOTS, 2, CROSS_ROWS, LANES), narrow),
             pltpu.VMEM((CROSS, 2, CROSS_ROWS, LANES), narrow),

time: 124 us -> 121 us (0.976)
  the two profiles are of different devices: /device:TPU:39 before, /device:TPU:4 now
where the time goes in v4:
time: 121 us; the launch traced here: 120 us
  Pallas kernels  117 us (97%)
  local copies, waits for them, and re-layouts  2.54 us (2%)
    pallas_call x1, Pallas kernels, per_device(): pl.pallas_call(functools.partial(kernel, n_blk), out_shape=(jax.ShapeDtyp...  117 us

profile of v4, /device:TPU:4, one launch (start us, length us, event | category | flops | bytes accessed | tf_op | source)
XLA Modules:
  0.0 120.4 jit_solution(2583321492184639845)
XLA Ops:
  0.6 117.2 %shard_map.94 = (bf16[128,2048]{1,0:T(8,128)(2,1)}, bf16[2,128,512]{2,1,0:T(8,128)(2,1)}) custom-call(bf16[128,2048]{1,0:T(8,128)(2,1)} %query_in.1, bf16[128,2048]{1,0:T(8,128)(2,1)} %grad_in.1, bf16[128,512]{1,0:T(8,128)(2,1)} %key_in.1, bf16[128,512]{1,0:T(8,128)(2,1)} %value_in.1, bf16[128,2048]{1,0:T(8,128)(2,1)} %out_in.1, f32[32,128]{1,0:T(8,128)} %bitcast.5, ...), custom_call_target="tpu_custom_call" | custom-call | tf_op jit(solution)/shard_map/pallas_call | solution.py:389
  117.9 0.0 copy-start
  117.9 1.7 %slice_bitcast_fusion = (bf16[128,512]{1,0:T(8,128)(2,1)}, bf16[128,512]{1,0:T(8,128)(2,1)}) fusion(bf16[2,128,512]{2,1,0:T(8,128)(2,1)} %get-tuple-element.6), kind=kLoop, calls=%fused_computation | loop fusion | bytes 524288 | tf_op jit(solution)/shard_map/squeeze | solution.py:432
  119.6 0.0 copy-done
  119.6 0.8 copy.11
Async XLA Ops:
  117.9 1.8 %copy-start = (bf16[128,2048]{1,0:T(8,128)(2,1)S(1)}, bf16[128,2048]{1,0:T(8,128)(2,1)}, u32[]{:S(2)}) copy-start(bf16[128,2048]{1,0:T(8,128)(2,1)} %get-tuple-element.12) | copy-start | bytes 1572868

commit v5 on v4

--- a/solution.py
+++ b/solution.py
@@ -18,7 +18,7 @@
 WIDTH = HEADS_LOCAL * HEAD_DIM
 CROSS = 16
 CROSS_ROWS = HALF // CROSS
-AHEAD = 5
+AHEAD = 6
 SLOTS = CROSS + AHEAD
 NEAR_ROWS = 128
 EARLY = 2

time: 121 us -> 119 us (0.983)
  the two profiles are of different devices: /device:TPU:4 before, /device:TPU:7 now
where the time goes in v5:
time: 119 us; the launch traced here: 118 us
  Pallas kernels  115 us (97%)
  local copies, waits for them, and re-layouts  2.54 us (2%)
    pallas_call x1, Pallas kernels, per_device(): pl.pallas_call(functools.partial(kernel, n_blk), out_shape=(jax.ShapeDtyp...  115 us

profile of v5, /device:TPU:7, one launch (start us, length us, event | category | flops | bytes accessed | tf_op | source)
XLA Modules:
  0.0 118.3 jit_solution(7536363337368256650)
XLA Ops:
  0.6 115.1 %shard_map.94 = (bf16[128,2048]{1,0:T(8,128)(2,1)}, bf16[2,128,512]{2,1,0:T(8,128)(2,1)}) custom-call(bf16[128,2048]{1,0:T(8,128)(2,1)} %query_in.1, bf16[128,2048]{1,0:T(8,128)(2,1)} %grad_in.1, bf16[128,512]{1,0:T(8,128)(2,1)} %key_in.1, bf16[128,512]{1,0:T(8,128)(2,1)} %value_in.1, bf16[128,2048]{1,0:T(8,128)(2,1)} %out_in.1, f32[32,128]{1,0:T(8,128)} %bitcast.5, ...), custom_call_target="tpu_custom_call" | custom-call | tf_op jit(solution)/shard_map/pallas_call | solution.py:389
  115.7 0.0 copy-start
  115.7 1.7 %slice_bitcast_fusion = (bf16[128,512]{1,0:T(8,128)(2,1)}, bf16[128,512]{1,0:T(8,128)(2,1)}) fusion(bf16[2,128,512]{2,1,0:T(8,128)(2,1)} %get-tuple-element.6), kind=kLoop, calls=%fused_computation | loop fusion | bytes 524288 | tf_op jit(solution)/shard_map/squeeze | solution.py:432
  117.5 0.0 copy-done
  117.5 0.8 copy.11
Async XLA Ops:
  115.7 1.8 %copy-start = (bf16[128,2048]{1,0:T(8,128)(2,1)S(1)}, bf16[128,2048]{1,0:T(8,128)(2,1)}, u32[]{:S(2)}) copy-start(bf16[128,2048]{1,0:T(8,128)(2,1)} %get-tuple-element.12) | copy-start | bytes 1572868
